TPU v7x, 32 devices: a whole 2x2x4 slice. The times are simulated.
32 devices in a mesh: feat: 8 (over z, core), node: 4 (over y, x).
Axes of the slice: x: 2, y: 2, z: 4, core: 2. Of those that a mesh axis runs over, the one named last changes fastest.
Arguments:
- node_features: bfloat16 [1024, 4, 1024], P('feat', 'node'), may hold values from -6 to 6
- weight: bfloat16 [1024, 256], P('feat'), may hold values from -0.1875 to 0.1875
- out_bias: float32 [256], replicated, may hold values from -3 to 3
- edge_tiles: bfloat16 [4, 8, 8, 128, 128], P('node', 'feat'), may hold values from 0.049804688 to 1
- tile_column: int32 [4, 8, 8], P('node', 'feat'), may hold values from 0 to 7, as said below
- tile_count: int32 [4, 8], P('node', 'feat'), may hold values from 1 to 8, as said below
- grad_hidden: bfloat16 [4, 1024, 256], P('node', 'feat'), may hold values from -6 to 6
Outputs:
- hidden: bfloat16 [4, 1024, 256], P('node', 'feat')
- grad_features: bfloat16 [1024, 4, 1024], P('feat', 'node')
- weight_grad: float32 [1024, 256], P('feat')
Inputs may be any that keep to these rules, and one draw needn't show every extreme that they name: `tile_column`: the 8 column blocks listed for one row block are distinct, live slots or not. `tile_count`: slots of a row block beyond its count are ignored. In every cluster some row block has exactly 8 live tiles.
All inputs are finite; a program needn't handle non-finite values.
Results may differ from a plain program's by a relative error of at most 0.007.
Values may be sent and summed in bfloat16 or wider, within the bound.
A program may use at most 64 MiB of HBM per device.

v0:
```python
import math
import jax
import jax.numpy as jnp
from jax import lax
from jax.sharding import PartitionSpec as P


def gelu_tanh(pre_value):
    return jax.nn.gelu(pre_value, approximate=True)


def body(node_features, weight, out_bias, edge_tiles, tile_column, tile_count, grad_hidden):
    feat_dev, clusters, cluster_rows = node_features.shape
    blocks = lax.axis_size("feat")
    tile_rows = cluster_rows // blocks
    hidden_width = weight.shape[1]
    summed_rows = lax.psum_scatter(
        jnp.einsum("fqr,fh->rqh", node_features, weight, preferred_element_type=jnp.float32),
        "feat",
        scatter_dimension=0,
        tiled=True,
    )
    own_proj = jnp.transpose(summed_rows, (1, 0, 2))
    own_rounded = own_proj.astype(jnp.bfloat16)
    all_proj = lax.all_gather(own_rounded, "feat", axis=1, tiled=True)
    blocks_proj = all_proj.reshape(clusters, blocks, tile_rows, hidden_width)
    my_tiles = edge_tiles[:, 0]
    my_cols = tile_column[:, 0]
    counts = tile_count[:, 0]
    slot_ids = jnp.arange(my_tiles.shape[1], dtype=jnp.int32)
    live_mask = (slot_ids[None, :] < counts[:, None]).astype(jnp.bfloat16)
    masked = my_tiles * live_mask[:, :, None, None]
    degree = jnp.sum(masked, axis=(1, 3), dtype=jnp.float32)
    cluster_ids = jnp.arange(clusters, dtype=jnp.int32)[:, None]
    chosen = blocks_proj[cluster_ids, my_cols]
    summed = jnp.einsum("qsij,qsjh->qih", masked, chosen, preferred_element_type=jnp.float32)
    row_scale = lax.rsqrt(degree)[:, :, None]
    pre_act = summed * row_scale + out_bias
    activated, backward = jax.vjp(gelu_tanh, pre_act)
    hidden = activated.astype(jnp.bfloat16)
    (grad_pre,) = backward(grad_hidden.astype(jnp.float32))
    scaled = (grad_pre * row_scale).astype(jnp.bfloat16)
    tile_terms = jnp.einsum(
        "qsij,qih->qsjh", masked, scaled, preferred_element_type=jnp.float32
    ).astype(jnp.bfloat16)
    outgoing = (
        jnp.zeros((blocks, clusters, tile_rows, hidden_width), jnp.bfloat16)
        .at[my_cols, cluster_ids]
        .set(tile_terms)
    )
    arrived = lax.all_to_all(outgoing, "feat", split_axis=0, concat_axis=0, tiled=True)
    own_grad = jnp.sum(arrived, axis=0, dtype=jnp.float32).astype(jnp.bfloat16)
    all_grad = lax.all_gather(own_grad, "feat", axis=1, tiled=True)
    grad_features = jnp.einsum(
        "fh,qrh->fqr", weight, all_grad, preferred_element_type=jnp.float32
    ).astype(jnp.bfloat16)
    partial_grad = jnp.einsum(
        "fqr,qrh->fh", node_features, all_grad, preferred_element_type=jnp.float32
    )
    total_nodes = clusters * lax.axis_size("node") * cluster_rows
    weight_grad = lax.psum(partial_grad, "node") * (1.0 / math.sqrt(total_nodes))
    return (hidden, grad_features, weight_grad)


def solution(mesh):
    return jax.shard_map(
        body,
        mesh=mesh,
        in_specs=(
            P("feat", "node", None),
            P("feat", None),
            P(),
            P("node", "feat", None, None, None),
            P("node", "feat", None),
            P("node", "feat"),
            P("node", "feat", None),
        ),
        out_specs=(P("node", "feat", None), P("feat", "node", None), P("feat", None)),
        check_vma=False,
    )
```

profile of v0, /device:TPU:0, one launch (start us, length us, event | category | flops | bytes accessed | tf_op | source)
XLA Modules:
  0.0 150.2 jit_solution(10850708865901555610)
XLA Ops:
  7.2 0.0 reduce-scatter.2.cloned.1.call-start
  7.2 0.9 copy-done
  8.1 2.1 %convolution_bitcast_fusion = f32[1024,1,256]{0,2,1:T(8,128)} fusion(bf16[128,256]{1,0:T(8,128)(2,1)} %param.8, bf16[128,1,1024]{2,0,1:T(8,128)(2,1)S(1)} %copy-done), kind=kOutput, calls=%fused_computation.2 | convolution fusion | flops 67108864 | bytes 1376256 | tf_op jit(solution)/shard_map/fqr,fh->rqh/dot_general | solution.py:18
  10.3 0.0 reduce-scatter.2.cloned.1.call-update
  11.0 0.2 copy-done.1
  11.2 0.2 convert_reduce_fusion
  11.4 0.6 copy-done.5
  12.1 33.3 %reduce-scatter.2.cloned.1.call-done = f32[128,1,256]{0,2,1:T(8,128)} async-done(((f32[1024,1,256]{0,2,1:T(8,128)}), f32[128,1,256]{0,2,1:T(8,128)}) %reduce-scatter.2.cloned.1.call-update) | async-done | bytes 131088 | tf_op jit(solution)/shard_map/reduce_scatter | solution.py:17
  45.5 0.9 convert_element_type.64
  46.4 14.0 %all-gather = bf16[1024,1,256]{0,2,1:T(8,128)(2,1)S(1)} all-gather(bf16[128,1,256]{0,2,1:T(8,128)(2,1)S(1)} %convert_element_type.64), channel_id=2, replica_groups=mesh['feat'=8,'node'=4] {'feat'}, dimensions={0}, use_global_device_ids=true | all-gather | bytes 589824 | tf_op jit(solution)/shard_map/all_gather | solution.py:25
  60.4 0.2 copy.22
  60.6 0.6 gather_fusion
  61.2 0.1 copy-done.3
  61.3 0.3 fusion.2
  61.5 0.6 copy-done.4
  62.1 0.4 convolution_convert_fusion
  62.5 0.8 broadcast.100
  63.4 2.5 %scatter_fusion = bf16[8,128,256]{2,1,0:T(8,128)(2,1)} fusion(bf16[8,128,256]{2,1,0:T(8,128)(2,1)} %broadcast.100, s32[8]{0:T(128)S(1)} %fusion.32, bf16[8,128,256]{2,1,0:T(8,128)(2,1)S(1)} %convolution_convert_fusion), kind=kCustom, calls=%fused_computation.1 | custom fusion | bytes 1572896 | tf_op jit(solution)/shard_map/scatter | solution.py:49
  65.8 3.5 %all-to-all-start = ((bf16[8,1,128,256]{3,2,1,0:T(8,128)(2,1)}), bf16[8,1,128,256]{3,2,1,0:T(8,128)(2,1)S(1)}, u32[]{:S(2)}, u32[]{:S(2)}) async-start(bf16[8,1,128,256]{3,2,1,0:T(8,128)(2,1)} %bitcast.21), calls=%async_computation.1 | async-start | bytes 1048576 | tf_op jit(solution)/shard_map/all_to_all | solution.py:51
  69.3 0.0 all-reduce.4.cloned.1.call-start
  69.4 0.7 fusion.31
  70.0 14.6 %all-to-all-done = bf16[8,1,128,256]{3,2,1,0:T(8,128)(2,1)S(1)} async-done(((bf16[8,1,128,256]{3,2,1,0:T(8,128)(2,1)}), bf16[8,1,128,256]{3,2,1,0:T(8,128)(2,1)S(1)}, u32[]{:S(2)}, u32[]{:S(2)}) %all-to-all-start) | async-done | bytes 524320 | tf_op jit(solution)/shard_map/all_to_all | solution.py:51
  84.6 0.1 reduce_sum.24
  84.7 14.9 %all-gather.1 = bf16[1024,256]{1,0:T(8,128)(2,1)S(1)} all-gather(bf16[128,256]{1,0:T(8,128)(2,1)S(1)} %reduce_sum.24), channel_id=3, replica_groups=mesh['feat'=8,'node'=4] {'feat'}, dimensions={0}, use_global_device_ids=true | all-gather | bytes 589824 | tf_op jit(solution)/shard_map/all_gather | solution.py:53
  99.6 1.0 convolution_bitcast_fusion.1
  100.6 0.0 all-reduce.4.cloned.1.call-update
  100.6 0.8 copy-done.2
  101.5 0.3 fusion
  101.8 0.9 copy.19
  102.6 39.1 %all-reduce.4.cloned.1.call-done = f32[128,256]{0,1:T(8,128)} async-done(((f32[128,256]{0,1:T(8,128)}), f32[128,256]{0,1:T(8,128)}) %all-reduce.4.cloned.1.call-update) | async-done | bytes 131088 | tf_op jit(solution)/shard_map/psum | solution.py:61
  141.7 0.9 broadcast_multiply_fusion
  142.6 0.8 copy.20
  (12 shorter events, 0.1 us)
Async XLA Ops:
  7.2 1.0 copy-start
  7.2 38.3 %reduce-scatter.2.cloned.1.call-start = ((), (), s32[]{:S(2)}) async-start(), calls=%async_computation.2 | async-start | bytes 1179648 | tf_op jit(solution)/shard_map/reduce_scatter | solution.py:17
  10.3 1.0 copy-start.1
  11.4 0.7 copy-start.5
  60.6 0.7 copy-start.3
  61.3 0.8 copy-start.4
  65.8 18.8 %all-to-all-start = ((bf16[8,1,128,256]{3,2,1,0:T(8,128)(2,1)}), bf16[8,1,128,256]{3,2,1,0:T(8,128)(2,1)S(1)}, u32[]{:S(2)}, u32[]{:S(2)}) async-start(bf16[8,1,128,256]{3,2,1,0:T(8,128)(2,1)} %bitcast.21), calls=%async_computation.1 | async-start | bytes 1048576 | tf_op jit(solution)/shard_map/all_to_all | solution.py:51
  69.3 72.4 %all-reduce.4.cloned.1.call-start = ((), (), s32[]{:S(2)}) async-start(), calls=%async_computation.3 | async-start | bytes 262144 | tf_op jit(solution)/shard_map/psum | solution.py:61
  100.6 0.8 copy-start.2
Sparse Core Ops, SparseCore 0:
  10.4 35.0 reduce-scatter.1
  100.8 40.8 all-reduce.3
where the time goes:
time: 151 us; the launch traced here: 150 us
  waiting for transfers between devices  87 us (58%)
  blocking collectives  28.9 us (19%)
  between operations  14.8 us (10%)
  local copies, waits for them, and re-layouts  8.93 us (6%)
  matrix products  4.12 us (3%)
  starting transfers between devices  3.57 us (2%)
  other arithmetic  2.8 us (2%)
    psum x1, waiting for transfers between devices, body(): lax.psum(partial_grad, 'node') * (1.0 / math.sqrt(total_nodes))  39.1 us
    reduce_scatter x1, waiting for transfers between devices, body(): lax.psum_scatter(jnp.einsum('fqr,fh->rqh', node_features, weight, preferr...  33.3 us
    all_gather x1, blocking collectives, body(): all_grad = lax.all_gather(own_grad, 'feat', axis=1, tiled=True)  14.9 us
    all_to_all x1, waiting for transfers between devices, body(): lax.all_to_all(outgoing, 'feat', split_axis=0, concat_axis=0, tiled=True)  14.6 us
    all_gather x1, blocking collectives, body(): all_proj = lax.all_gather(own_rounded, 'feat', axis=1, tiled=True)  14 us
    unnamed x14, local copies, waits for them, and re-layouts  4.86 us
    all_to_all x1, starting transfers between devices, body(): lax.all_to_all(outgoing, 'feat', split_axis=0, concat_axis=0, tiled=True)  3.49 us
  transfers between devices with their start and end apart: 3, of which 3 were waited for; matrix products, arithmetic and copies ran while one was open for 1% of the time, Pallas kernels for 0%

commit v1 on v0

--- a/solution.py
+++ b/solution.py
@@ -58,7 +58,9 @@
         "fqr,qrh->fh", node_features, all_grad, preferred_element_type=jnp.float32
     )
     total_nodes = clusters * lax.axis_size("node") * cluster_rows
-    weight_grad = lax.psum(partial_grad, "node") * (1.0 / math.sqrt(total_nodes))
+    weight_grad = jnp.sum(lax.all_gather(partial_grad, "node"), axis=0) * (
+        1.0 / math.sqrt(total_nodes)
+    )
     return (hidden, grad_features, weight_grad)
 
 

time: 151 us -> 125 us (0.83)
  waiting for transfers between devices: 87 us -> 48 us
  blocking collectives: 28.9 us -> 43.7 us
    psum x1 -> x0, waiting for transfers between devices: 39.1 us -> none  [body(): lax.psum(partial_grad, 'node') * (1.0 / math.sqrt(total_nodes))]
    all_gather x0 -> x1, blocking collectives: none -> 14.6 us  [body(): lax.all_gather(partial_grad, 'node')]
  transfers between devices with their start and end apart: 3 -> 2, of which waited for: 3 -> 2; matrix products, arithmetic and copies ran while one was open for 1% -> 1% of each run, Pallas kernels for 0% -> 0%
where the time goes in v1:
time: 125 us; the launch traced here: 124 us
  waiting for transfers between devices  48 us (38%)
  blocking collectives  43.7 us (35%)
  between operations  14.8 us (12%)
  local copies, waits for them, and re-layouts  8.32 us (7%)
  starting transfers between devices  3.53 us (3%)
  matrix products  3.48 us (3%)
  other arithmetic  2.21 us (2%)
    reduce_scatter x1, waiting for transfers between devices, body(): lax.psum_scatter(jnp.einsum('fqr,fh->rqh', node_features, weight, preferr...  33.3 us
    all_gather x1, blocking collectives, body(): all_grad = lax.all_gather(own_grad, 'feat', axis=1, tiled=True)  15.1 us
    all_gather x1, blocking collectives, body(): lax.all_gather(partial_grad, 'node')  14.6 us
    all_to_all x1, waiting for transfers between devices, body(): lax.all_to_all(outgoing, 'feat', split_axis=0, concat_axis=0, tiled=True)  14.6 us
    all_gather x1, blocking collectives, body(): all_proj = lax.all_gather(own_rounded, 'feat', axis=1, tiled=True)  14 us
    unnamed x14, local copies, waits for them, and re-layouts  4.05 us
    all_to_all x1, starting transfers between devices, body(): lax.all_to_all(outgoing, 'feat', split_axis=0, concat_axis=0, tiled=True)  3.49 us
  transfers between devices with their start and end apart: 2, of which 2 were waited for; matrix products, arithmetic and copies ran while one was open for 1% of the time, Pallas kernels for 0%

profile of v1, /device:TPU:0, one launch (start us, length us, event | category | flops | bytes accessed | tf_op | source)
XLA Modules:
  0.0 124.0 jit_solution(9725458275251633817)
XLA Ops:
  7.2 0.0 copy-start
  7.2 0.0 reduce-scatter.2.cloned.1.call-start
  7.2 0.9 copy-done
  8.1 2.1 %convolution_bitcast_fusion = f32[1024,1,256]{0,2,1:T(8,128)} fusion(bf16[128,256]{1,0:T(8,128)(2,1)} %param.8, bf16[128,1,1024]{2,0,1:T(8,128)(2,1)S(1)} %copy-done), kind=kOutput, calls=%fused_computation.2 | convolution fusion | flops 67108864 | bytes 1376256 | tf_op jit(solution)/shard_map/fqr,fh->rqh/dot_general | solution.py:18
  10.3 0.0 reduce-scatter.2.cloned.1.call-update
  11.0 0.2 copy-done.1
  11.2 0.2 convert_reduce_fusion
  11.4 0.6 copy-done.5
  12.1 33.3 %reduce-scatter.2.cloned.1.call-done = f32[128,1,256]{0,2,1:T(8,128)} async-done(((f32[1024,1,256]{0,2,1:T(8,128)}), f32[128,1,256]{0,2,1:T(8,128)}) %reduce-scatter.2.cloned.1.call-update) | async-done | bytes 131088 | tf_op jit(solution)/shard_map/reduce_scatter | solution.py:17
  45.5 0.9 convert_element_type.64
  46.4 14.0 %all-gather = bf16[1024,1,256]{0,2,1:T(8,128)(2,1)S(1)} all-gather(bf16[128,1,256]{0,2,1:T(8,128)(2,1)S(1)} %convert_element_type.64), channel_id=2, replica_groups=mesh['feat'=8,'node'=4] {'feat'}, dimensions={0}, use_global_device_ids=true | all-gather | bytes 589824 | tf_op jit(solution)/shard_map/all_gather | solution.py:25
  60.4 0.2 copy.20
  60.6 0.0 copy-start.3
  60.6 0.6 gather_fusion
  61.2 0.1 copy-done.3
  61.3 0.3 fusion.2
  61.6 0.6 copy-done.4
  62.1 0.4 convolution_convert_fusion
  62.5 0.8 broadcast.100
  63.4 2.5 %scatter_fusion = bf16[8,128,256]{2,1,0:T(8,128)(2,1)} fusion(bf16[8,128,256]{2,1,0:T(8,128)(2,1)} %broadcast.100, s32[8]{0:T(128)S(1)} %fusion.32, bf16[8,128,256]{2,1,0:T(8,128)(2,1)S(1)} %convolution_convert_fusion), kind=kCustom, calls=%fused_computation.1 | custom fusion | bytes 1572896 | tf_op jit(solution)/shard_map/scatter | solution.py:49
  65.8 3.5 %all-to-all-start = ((bf16[8,1,128,256]{3,2,1,0:T(8,128)(2,1)}), bf16[8,1,128,256]{3,2,1,0:T(8,128)(2,1)S(1)}, u32[]{:S(2)}, u32[]{:S(2)}) async-start(bf16[8,1,128,256]{3,2,1,0:T(8,128)(2,1)} %bitcast.21), calls=%async_computation.1 | async-start | bytes 1048576 | tf_op jit(solution)/shard_map/all_to_all | solution.py:51
  69.3 0.7 fusion.31
  70.0 14.6 %all-to-all-done = bf16[8,1,128,256]{3,2,1,0:T(8,128)(2,1)S(1)} async-done(((bf16[8,1,128,256]{3,2,1,0:T(8,128)(2,1)}), bf16[8,1,128,256]{3,2,1,0:T(8,128)(2,1)S(1)}, u32[]{:S(2)}, u32[]{:S(2)}) %all-to-all-start) | async-done | bytes 524320 | tf_op jit(solution)/shard_map/all_to_all | solution.py:51
  84.6 0.1 reduce_sum.33
  84.7 15.1 %all-gather.1 = bf16[1024,256]{1,0:T(8,128)(2,1)S(1)} all-gather(bf16[128,256]{1,0:T(8,128)(2,1)S(1)} %reduce_sum.33), channel_id=3, replica_groups=mesh['feat'=8,'node'=4] {'feat'}, dimensions={0}, use_global_device_ids=true | all-gather | bytes 589824 | tf_op jit(solution)/shard_map/all_gather | solution.py:53
  99.8 0.3 fusion
  100.1 0.3 convolution_bitcast_fusion.1
  100.4 0.9 copy.17
  101.3 14.6 %all-gather.2 = f32[512,256]{0,1:T(8,128)S(1)} all-gather(f32[128,256]{0,1:T(8,128)S(1)} %convolution_bitcast_fusion.1), channel_id=4, replica_groups=mesh['feat'=8,'node'=4] {'node'}, dimensions={0}, use_global_device_ids=true | all-gather | bytes 655360 | tf_op jit(solution)/shard_map/all_gather | solution.py:61
  115.9 0.2 reshape.170
  116.1 0.3 reduce_sum.35
  116.4 0.8 copy.18
  (12 shorter events, 0.1 us)
Async XLA Ops:
  7.2 1.0 copy-start
  7.2 38.3 %reduce-scatter.2.cloned.1.call-start = ((), (), s32[]{:S(2)}) async-start(), calls=%async_computation.2 | async-start | bytes 1179648 | tf_op jit(solution)/shard_map/reduce_scatter | solution.py:17
  10.3 1.0 copy-start.1
  11.4 0.7 copy-start.5
  60.6 0.7 copy-start.3
  61.3 0.8 copy-start.4
  65.8 18.8 %all-to-all-start = ((bf16[8,1,128,256]{3,2,1,0:T(8,128)(2,1)}), bf16[8,1,128,256]{3,2,1,0:T(8,128)(2,1)S(1)}, u32[]{:S(2)}, u32[]{:S(2)}) async-start(bf16[8,1,128,256]{3,2,1,0:T(8,128)(2,1)} %bitcast.21), calls=%async_computation.1 | async-start | bytes 1048576 | tf_op jit(solution)/shard_map/all_to_all | solution.py:51
  84.7 15.1 %copy-start.2 = (bf16[128,256]{1,0:T(8,128)(2,1)S(1)}, bf16[128,256]{1,0:T(8,128)(2,1)}, u32[]{:S(2)}) copy-start(bf16[128,256]{1,0:T(8,128)(2,1)} %param.8) | copy-start | bytes 196612
Sparse Core Ops, SparseCore 0:
  10.4 35.0 reduce-scatter.1
